TPU v7x, 32 devices: a whole 2x2x4 slice. The times are simulated.
32 devices in a mesh: seq: 8 (over z, y), rep: 4 (over x, core).
Axes of the slice: x: 2, y: 2, z: 4, core: 2. Of those that a mesh axis runs over, the one named last changes fastest.
Arguments:
- queries: bfloat16 [4, 2048, 512], P('rep', 'seq'), may hold values from -6 to 6
- key_vectors: bfloat16 [4, 2048, 128], P('rep', 'seq'), may hold values from -6 to 6
- values: bfloat16 [4, 2048, 128], P('rep', 'seq'), may hold values from -6 to 6
- forget_logit: bfloat16 [4, 4, 2048], P('rep', None, 'seq'), may hold values from 0 to 11
- out_grad: bfloat16 [4, 2048, 512], P('rep', 'seq'), may hold values from -6 to 6
- query_gain: float32 [128], replicated, may hold values from 0.1 to 1.9
- key_gain: float32 [128], replicated, may hold values from 0.1 to 1.9
- lengths: int32 [4, 4], P('rep'), may hold values from 1 to 24, 32 in all within a row
Outputs:
- attention: bfloat16 [4, 2048, 512], P('rep', 'seq')
- query_grad: bfloat16 [4, 2048, 512], P('rep', 'seq')
- key_grad: bfloat16 [4, 2048, 128], P('rep', 'seq')
- value_grad: bfloat16 [4, 2048, 128], P('rep', 'seq')
- forget_grad: float32 [4, 4, 2048], P('rep', None, 'seq')
- norm_gain_grad: float32 [2, 128], replicated
Inputs may be any that keep to these rules, and one draw needn't show every extreme that they name: `lengths`: each row lists the documents of one pack in order, in tiles of 64 tokens, and sums to 32.
All inputs are finite; a program needn't handle non-finite values.
Results may differ from a plain program's by a relative error of at most 0.02.
Values may be sent and summed in bfloat16 or wider, within the bound.
No kernel may reach another device: no remote copies, remote signals or barrier semaphores. Data moves between devices by JAX's collectives and lax.ppermute only.
A program may use at most 64 MiB of HBM per device.

v0:
```python
import jax
import jax.numpy as jnp
from jax import lax
from jax.sharding import PartitionSpec as P

TILE = 64
norm_eps = 1e-06
key_span = 512


def shifted(value, axis, steps):
    count = lax.axis_size(axis)
    initial, last = (max(0, -steps), min(count, count - steps))
    return lax.ppermute(value, axis, [(source, source + steps) for source in range(initial, last)])


def norm_rows(raw_values, gain_vec, factor):
    lifted = raw_values.astype(jnp.float32)
    mean_square = jnp.mean(lifted * lifted, axis=-1, keepdims=True)
    return lifted * lax.rsqrt(mean_square + norm_eps) * (gain_vec * factor)


def tile_starts(lengths_row, tile_count):
    doc_ends = jnp.cumsum(lengths_row)
    tile_index = jnp.arange(tile_count, dtype=jnp.int32)
    passed = doc_ends[None, :] <= tile_index[:, None]
    return jnp.sum(jnp.where(passed, lengths_row[None, :], 0), axis=1)


def pad_rows(array_in, along):
    widths = [(0, 0)] * array_in.ndim
    widths[along] = (0, key_span)
    return jnp.pad(array_in, widths)


def prepare(gathered):
    key_all, value_all, logit_all = gathered
    gate = jnp.cumsum(jax.nn.log_sigmoid(logit_all.astype(jnp.float32)), axis=1)
    return (pad_rows(key_all, 0), pad_rows(value_all, 0), pad_rows(gate, 1))


def contract_last(left_rows, right_rows):
    return lax.dot_general(
        left_rows, right_rows, (((1,), (1,)), ((), ())), preferred_element_type=jnp.float32
    )


def contract_first(left_rows, right_rows):
    return lax.dot_general(
        left_rows, right_rows, (((0,), (0,)), ((), ())), preferred_element_type=jnp.float32
    )


def block_scores(
    query_rows, key_pad, gate_pad, query_gate, block_first, tile_first, doc_first, head_count
):
    key_block = lax.dynamic_slice_in_dim(key_pad, block_first, key_span, 0)
    scores = contract_last(query_rows, key_block)
    row_count = query_rows.shape[0] // head_count
    scores = scores.reshape(head_count, row_count, key_span)
    key_gate = lax.dynamic_slice_in_dim(gate_pad, block_first, key_span, 1)
    scores = scores + query_gate[:, :, None] - key_gate[:, None, :]
    key_place = block_first + jnp.arange(key_span, dtype=jnp.int32)
    query_place = tile_first + jnp.arange(row_count, dtype=jnp.int32)
    allowed = (key_place[None, :] >= doc_first) & (key_place[None, :] <= query_place[:, None])
    return (jnp.where(allowed[None, :, :], scores, -jnp.inf), key_block)


def query_setup(query_tile, tile_id, doc_tile, gate_pad, query_gain, head_count, head_dim):
    row_count = query_tile.shape[0]
    scale_factor = head_dim ** (-0.5)
    normed = norm_rows(
        query_tile.reshape(row_count, head_count, head_dim), query_gain, scale_factor
    ).astype(jnp.bfloat16)
    query_rows = normed.transpose(1, 0, 2).reshape(head_count * row_count, head_dim)
    tile_first = tile_id * row_count
    doc_first = doc_tile * row_count
    query_gate = lax.dynamic_slice_in_dim(gate_pad, tile_first, row_count, 1)
    block_count = (tile_first + row_count - doc_first + key_span - 1) // key_span
    return (query_rows, tile_first, doc_first, query_gate, block_count)


def forward_task(
    query_tile, tile_id, doc_tile, key_pad, value_pad, gate_pad, query_gain, head_count
):
    row_count, full_width = query_tile.shape
    head_dim = key_pad.shape[1]
    query_rows, tile_first, doc_first, query_gate, block_count = query_setup(
        query_tile, tile_id, doc_tile, gate_pad, query_gain, head_count, head_dim
    )

    def block_step(block_index, loop_state):
        row_total, value_sum = loop_state
        block_first = doc_first + block_index * key_span
        scores, key_block = block_scores(
            query_rows,
            key_pad,
            gate_pad,
            query_gate,
            block_first,
            tile_first,
            doc_first,
            head_count,
        )
        weights = jnp.exp(scores)
        value_block = lax.dynamic_slice_in_dim(value_pad, block_first, key_span, 0)
        mixed_rows = jnp.dot(
            weights.reshape(head_count * row_count, key_span).astype(jnp.bfloat16),
            value_block,
            preferred_element_type=jnp.float32,
        )
        return (row_total + jnp.sum(weights, axis=2), value_sum + mixed_rows)

    start_state = (
        jnp.zeros((head_count, row_count), jnp.float32),
        jnp.zeros((head_count * row_count, head_dim), jnp.float32),
    )
    row_total, value_sum = lax.fori_loop(0, block_count, block_step, start_state)
    result = value_sum.reshape(head_count, row_count, head_dim) / row_total[:, :, None]
    return result.transpose(1, 0, 2).reshape(row_count, full_width).astype(jnp.bfloat16)


def backward_task(
    partials,
    query_tile,
    grad_tile,
    out_tile,
    tile_id,
    doc_tile,
    key_pad,
    value_pad,
    gate_pad,
    query_gain,
    head_count,
):
    row_count, full_width = query_tile.shape
    head_dim = key_pad.shape[1]
    query_rows, tile_first, doc_first, query_gate, block_count = query_setup(
        query_tile, tile_id, doc_tile, gate_pad, query_gain, head_count, head_dim
    )
    grad_rows = (
        grad_tile.reshape(row_count, head_count, head_dim)
        .transpose(1, 0, 2)
        .reshape(head_count * row_count, head_dim)
    )
    product = grad_tile.astype(jnp.float32) * out_tile.astype(jnp.float32)
    out_inner = jnp.sum(product.reshape(row_count, head_count, head_dim), axis=2).T

    def total_step(block_index, row_total):
        block_first = doc_first + block_index * key_span
        scores, key_block = block_scores(
            query_rows,
            key_pad,
            gate_pad,
            query_gate,
            block_first,
            tile_first,
            doc_first,
            head_count,
        )
        return row_total + jnp.sum(jnp.exp(scores), axis=2)

    row_total = lax.fori_loop(
        0, block_count, total_step, jnp.zeros((head_count, row_count), jnp.float32)
    )

    def grad_step(block_index, loop_state):
        key_part, value_part, gate_part, query_grad, row_sum = loop_state
        block_first = doc_first + block_index * key_span
        scores, key_block = block_scores(
            query_rows,
            key_pad,
            gate_pad,
            query_gate,
            block_first,
            tile_first,
            doc_first,
            head_count,
        )
        probability = jnp.exp(scores) / row_total[:, :, None]
        value_block = lax.dynamic_slice_in_dim(value_pad, block_first, key_span, 0)
        prob_grad = contract_last(grad_rows, value_block).reshape(head_count, row_count, key_span)
        score_grad = probability * (prob_grad - out_inner[:, :, None])
        score_low = score_grad.reshape(head_count * row_count, key_span).astype(jnp.bfloat16)
        prob_low = probability.reshape(head_count * row_count, key_span).astype(jnp.bfloat16)
        query_grad = query_grad + jnp.dot(score_low, key_block, preferred_element_type=jnp.float32)
        key_update = contract_first(score_low, query_rows)
        value_update = contract_first(prob_low, grad_rows)
        key_part = lax.dynamic_update_slice_in_dim(
            key_part,
            lax.dynamic_slice_in_dim(key_part, block_first, key_span, 0) + key_update,
            block_first,
            0,
        )
        value_part = lax.dynamic_update_slice_in_dim(
            value_part,
            lax.dynamic_slice_in_dim(value_part, block_first, key_span, 0) + value_update,
            block_first,
            0,
        )
        column_sum = jnp.sum(score_grad, axis=1)
        gate_part = lax.dynamic_update_slice_in_dim(
            gate_part,
            lax.dynamic_slice_in_dim(gate_part, block_first, key_span, 1) - column_sum,
            block_first,
            1,
        )
        return (key_part, value_part, gate_part, query_grad, row_sum + jnp.sum(score_grad, axis=2))

    start_state = (
        partials[0],
        partials[1],
        partials[2],
        jnp.zeros((head_count * row_count, head_dim), jnp.float32),
        jnp.zeros((head_count, row_count), jnp.float32),
    )
    key_part, value_part, gate_part, query_grad, row_sum = lax.fori_loop(
        0, block_count, grad_step, start_state
    )
    gate_part = lax.dynamic_update_slice_in_dim(
        gate_part,
        lax.dynamic_slice_in_dim(gate_part, tile_first, row_count, 1) + row_sum,
        tile_first,
        1,
    )
    query_result = (
        query_grad.reshape(head_count, row_count, head_dim)
        .transpose(1, 0, 2)
        .reshape(row_count, full_width)
        .astype(jnp.bfloat16)
    )
    return ((key_part, value_part, gate_part), query_result)


def on_device(queries, key_vectors, values, forget_logit, out_grad, query_gain, key_gain, lengths):
    query_local = queries[0]
    key_local = key_vectors[0]
    value_local = values[0]
    logit_local = forget_logit[0]
    grad_local = out_grad[0]
    row_count, full_width = query_local.shape
    head_dim = key_local.shape[1]
    head_count = full_width // head_dim
    tile_dev = row_count // TILE
    servers = lax.axis_size("seq")
    owner_index = lax.axis_index("seq")
    tile_count = servers * tile_dev
    token_count = tile_count * TILE
    starts = tile_starts(lengths[0], tile_count)
    key_normed = norm_rows(key_local, key_gain, 1.0).astype(jnp.bfloat16)
    pads = prepare(
        (
            lax.all_gather(key_normed, "seq", axis=0, tiled=True),
            lax.all_gather(value_local, "seq", axis=0, tiled=True),
            lax.all_gather(logit_local, "seq", axis=1, tiled=True),
        )
    )
    lane_index = jnp.arange(tile_dev, dtype=jnp.int32)
    own_ids = owner_index * tile_dev + lane_index
    query_tiles = query_local.reshape(tile_dev, TILE, full_width)
    grad_tiles = grad_local.reshape(tile_dev, TILE, full_width)
    pad_set = pads
    out_tiles = lax.map(
        lambda task_item: forward_task(
            task_item[0],
            task_item[1],
            starts[task_item[1]],
            pad_set[0],
            pad_set[1],
            pad_set[2],
            query_gain,
            head_count,
        ),
        (query_tiles, own_ids),
    )
    pads = prepare(
        (
            lax.all_gather(key_normed, "seq", axis=0, tiled=True),
            lax.all_gather(value_local, "seq", axis=0, tiled=True),
            lax.all_gather(logit_local, "seq", axis=1, tiled=True),
        )
    )
    run_pad_set = pads
    zero_parts = (
        jnp.zeros(run_pad_set[0].shape, jnp.float32),
        jnp.zeros(run_pad_set[1].shape, jnp.float32),
        jnp.zeros(run_pad_set[2].shape, jnp.float32),
    )

    def task_step(partials, task_item):
        query_tile, grad_tile, out_tile, tile_id = task_item
        return backward_task(
            partials,
            query_tile,
            grad_tile,
            out_tile,
            tile_id,
            starts[tile_id],
            run_pad_set[0],
            run_pad_set[1],
            run_pad_set[2],
            query_gain,
            head_count,
        )

    partials, query_grad_tiles = lax.scan(
        task_step, zero_parts, (query_tiles, grad_tiles, out_tiles, own_ids)
    )
    key_part, value_part, gate_part = partials
    suffix = jnp.flip(jnp.cumsum(jnp.flip(gate_part[:, :token_count], 1), axis=1), 1)
    doc_most = tile_count * 3 // 4
    reach = min((doc_most + tile_dev - 2) // tile_dev, servers - 1)
    key_low = key_part[:token_count].astype(jnp.bfloat16)
    value_low = value_part[:token_count].astype(jnp.bfloat16)
    suffix_low = suffix.astype(jnp.bfloat16)

    def block_of(target):
        first_row = jnp.maximum(target, 0) * row_count
        return (
            lax.dynamic_slice_in_dim(key_low, first_row, row_count, 0),
            lax.dynamic_slice_in_dim(value_low, first_row, row_count, 0),
            lax.dynamic_slice_in_dim(suffix_low, first_row, row_count, 1),
        )

    own_block = block_of(owner_index)
    normed_key_grad = own_block[0].astype(jnp.float32)
    value_sum = own_block[1].astype(jnp.float32)
    gate_grad = own_block[2].astype(jnp.float32)
    for distance in range(1, reach + 1):
        piece = block_of(owner_index - distance)
        arrived_block = shifted((piece[0], piece[1], piece[2]), "seq", -distance)
        normed_key_grad = normed_key_grad + arrived_block[0].astype(jnp.float32)
        value_sum = value_sum + arrived_block[1].astype(jnp.float32)
        gate_grad = gate_grad + arrived_block[2].astype(jnp.float32)
    _, key_pullback = jax.vjp(
        lambda raw_values, gain_vec: norm_rows(raw_values, gain_vec, 1.0),
        key_local.astype(jnp.float32),
        key_gain,
    )
    key_input_grad, key_gain_part = key_pullback(normed_key_grad)
    scale_factor = head_dim ** (-0.5)
    _, query_pullback = jax.vjp(
        lambda raw_values, gain_vec: norm_rows(raw_values, gain_vec, scale_factor),
        query_local.reshape(row_count, head_count, head_dim).astype(jnp.float32),
        query_gain,
    )
    query_input_grad, query_gain_part = query_pullback(
        query_grad_tiles.reshape(row_count, head_count, head_dim).astype(jnp.float32)
    )
    forget_grad = gate_grad * jax.nn.sigmoid(-logit_local.astype(jnp.float32))
    gain_total = lax.psum(jnp.stack([query_gain_part, key_gain_part]), ("seq", "rep"))
    attention = out_tiles.reshape(row_count, full_width)
    return (
        attention[None],
        query_input_grad.reshape(row_count, full_width).astype(jnp.bfloat16)[None],
        key_input_grad.astype(jnp.bfloat16)[None],
        value_sum.astype(jnp.bfloat16)[None],
        forget_grad[None],
        gain_total,
    )


def solution(mesh):
    return jax.shard_map(
        on_device,
        mesh=mesh,
        in_specs=(
            P("rep", "seq", None),
            P("rep", "seq", None),
            P("rep", "seq", None),
            P("rep", None, "seq"),
            P("rep", "seq", None),
            P(),
            P(),
            P("rep", None),
        ),
        out_specs=(
            P("rep", "seq", None),
            P("rep", "seq", None),
            P("rep", "seq", None),
            P("rep", "seq", None),
            P("rep", None, "seq"),
            P(),
        ),
        check_vma=False,
    )
```

profile of v0, /device:TPU:12, one launch (start us, length us, event | category | flops | bytes accessed | tf_op | source)
XLA Modules:
  0.0 332.6 jit_solution(6965043462693032815)
XLA Ops:
  2.6 29.4 %all_gather.13 = bf16[2048,128]{1,0:T(8,128)(2,1)S(1)} all-gather(bf16[256,128]{1,0:T(8,128)(2,1)S(1)} %fusion.42), channel_id=1, replica_groups=mesh['seq'=8,'rep'=4] {'seq'}, dimensions={0}, use_global_device_ids=true | all-gather | bytes 589824 | tf_op jit(solution)/shard_map/all_gather | solution.py:253
  32.0 27.1 %all-gather = bf16[1,4,2048]{2,1,0:T(4,128)(2,1)S(1)} all-gather(bf16[1,4,256]{2,1,0:T(4,128)(2,1)} %param.21), channel_id=2, replica_groups=mesh['seq'=8,'rep'=4] {'seq'}, dimensions={2}, use_global_device_ids=true | all-gather | bytes 18432 | tf_op jit(solution)/shard_map/all_gather | solution.py:255
  60.8 28.6 %all-gather.1 = bf16[1,2048,128]{2,1,0:T(8,128)(2,1)S(1)} all-gather(bf16[1,256,128]{2,1,0:T(8,128)(2,1)} %param.20), channel_id=3, replica_groups=mesh['seq'=8,'rep'=4] {'seq'}, dimensions={1}, use_global_device_ids=true | all-gather | bytes 589824 | tf_op jit(solution)/shard_map/all_gather | solution.py:254
  90.5 33.2 %while.166 = (s32[]{:T(128)}, bf16[4,64,512]{2,1,0:T(8,128)(2,1)S(1)}, s32[4]{0:T(128)S(1)}, s32[32]{0:T(128)S(1)}, bf16[4,64,512]{2,1,0:T(8,128)(2,1)S(1)}, /*i...) while((s32[]{:T(128)}, ...), condition=%wide.region_10.11_spmd, body=%wide.region_5.10_spmd.sunk | while | flops 68126688 | bytes 5364638 | solution.py:263
  95.6 2.9 while.170
  104.0 2.9 while.170
  112.3 2.9 while.170
  120.6 2.9 while.170
  126.1 84.6 %while.169 = (s32[]{:T(128)}, f32[2560,128]{1,0:T(8,128)}, f32[2560,128]{1,0:T(8,128)}, f32[4,2560]{1,0:T(4,128)S(1)}, bf16[4,64,512]{2,1,0:T(8,128)(2,1)S(1)}, ...) while((s32[]{:T(128)}, f32[2560,128]{1,0:T(8,128)}, ...), condition=%wide.region_21.22_spmd, body=%wide.region_11.21_spmd.sunk | while | flops 204607008 | bytes 11740149 | solution.py:306
  131.3 2.3 while.171
  135.7 11.2 %while.172 = (s32[]{:T(128)}, f32[2560,128]{1,0:T(8,128)}, f32[2560,128]{1,0:T(8,128)}, f32[4,2560]{1,0:T(4,128)S(1)}, f32[256,128]{1,0:T(8,128)S(1)}, /*index=5...) while((s32[]{:T(128)}, f32[2560,128]{1,0:T(8,128)}, ...), condition=%wide.wide.region_20.20_spmd, body=%wide.wide.region_17.19_spmd.sunk | while | flops 170100288 | bytes 6100827 | solution.py:217
  152.4 2.3 while.171
  156.8 11.2 %while.172 = (s32[]{:T(128)}, f32[2560,128]{1,0:T(8,128)}, f32[2560,128]{1,0:T(8,128)}, f32[4,2560]{1,0:T(4,128)S(1)}, f32[256,128]{1,0:T(8,128)S(1)}, /*index=5...) while((s32[]{:T(128)}, f32[2560,128]{1,0:T(8,128)}, ...), condition=%wide.wide.region_20.20_spmd, body=%wide.wide.region_17.19_spmd.sunk | while | flops 170100288 | bytes 6100827 | solution.py:217
  173.6 2.3 while.171
  178.0 11.2 %while.172 = (s32[]{:T(128)}, f32[2560,128]{1,0:T(8,128)}, f32[2560,128]{1,0:T(8,128)}, f32[4,2560]{1,0:T(4,128)S(1)}, f32[256,128]{1,0:T(8,128)S(1)}, /*index=5...) while((s32[]{:T(128)}, f32[2560,128]{1,0:T(8,128)}, ...), condition=%wide.wide.region_20.20_spmd, body=%wide.wide.region_17.19_spmd.sunk | while | flops 170100288 | bytes 6100827 | solution.py:217
  194.7 2.3 while.171
  199.1 11.2 %while.172 = (s32[]{:T(128)}, f32[2560,128]{1,0:T(8,128)}, f32[2560,128]{1,0:T(8,128)}, f32[4,2560]{1,0:T(4,128)S(1)}, f32[256,128]{1,0:T(8,128)S(1)}, /*index=5...) while((s32[]{:T(128)}, f32[2560,128]{1,0:T(8,128)}, ...), condition=%wide.wide.region_20.20_spmd, body=%wide.wide.region_17.19_spmd.sunk | while | flops 170100288 | bytes 6100827 | solution.py:217
  230.7 8.8 %collective-permute-done.12 = bf16[4,256]{1,0:T(4,128)(2,1)S(1)} collective-permute-done((bf16[4,256]{1,0:T(4,128)(2,1)S(1)}, bf16[4,256]{1,0:T(4,128)(2,1)S(1)}, u32[]{:S(2)}, u32[]{:S(2)}) %collective-permute-start.12) | collective-permute-done | bytes 2080 | tf_op jit(solution)/shard_map/ppermute | solution.py:14
  240.1 19.3 %collective-permute-done.13 = bf16[4,256]{1,0:T(4,128)(2,1)S(1)} collective-permute-done((bf16[4,256]{1,0:T(4,128)(2,1)S(1)}, bf16[4,256]{1,0:T(4,128)(2,1)S(1)}, u32[]{:S(2)}, u32[]{:S(2)}) %collective-permute-start.13) | collective-permute-done | bytes 2080 | tf_op jit(solution)/shard_map/ppermute | solution.py:14
  260.1 2.0 collective-permute-done.14
  269.3 2.5 collective-permute-done.1
  276.6 4.1 %collective-permute-start.6 = (bf16[256,128]{1,0:T(8,128)(2,1)S(1)}, bf16[256,128]{1,0:T(8,128)(2,1)S(1)}, u32[]{:S(2)}, u32[]{:S(2)}) collective-permute-start(bf16[256,128]{1,0:T(8,128)(2,1)S(1)} %get-tuple-element.963), channel_id=1, source_target_pairs={{4,0},{8,4},{12,8},{16,12},{20,16},{24,20},{28,24},{5,1},{9,5},{13... | collective-permute-start | bytes 196616 | tf_op jit(solution)/shard_map/ppermute | solution.py:14
  280.7 3.2 collective-permute-start.7
  288.9 42.9 %psum.7 = f32[2,128]{1,0:T(2,128)} all-reduce(f32[2,128]{1,0:T(2,128)S(1)} %pad_maximum_fusion), channel_id=1, replica_groups=mesh['seq'=8,'rep'=4] {'seq','rep'}, use_global_device_ids=true, to_apply=%region_30.31 | all-reduce | flops 256 | bytes 2048 | tf_op jit(solution)/shard_map/psum | solution.py:351
  (641 shorter events, 134.7 us)
Async XLA Ops:
  0.6 88.8 %copy-start.9 = (s32[1,4]{1,0:T(1,128)S(1)}, s32[1,4]{1,0:T(1,128)}, u32[]{:S(2)}) copy-start(s32[1,4]{1,0:T(1,128)} %param.25) | copy-start | bytes 52
  210.8 15.1 %copy-start.4 = (bf16[4,64,512]{2,1,0:T(8,128)(2,1)}, bf16[4,64,512]{2,1,0:T(8,128)(2,1)S(1)}, u32[]{:S(2)}) copy-start(bf16[4,64,512]{2,1,0:T(8,128)(2,1)S(1)} %get-tuple-element.2002) | copy-start | bytes 786436
  212.2 13.6 %copy-start.3 = (bf16[2048,128]{1,0:T(8,128)(2,1)}, bf16[2048,128]{1,0:T(8,128)(2,1)S(1)}, u32[]{:S(2)}) copy-start(bf16[2048,128]{1,0:T(8,128)(2,1)S(1)} %slice.39) | copy-start | bytes 1572868
  212.2 55.8 %collective-permute-start = (bf16[256,128]{1,0:T(8,128)(2,1)S(1)}, bf16[256,128]{1,0:T(8,128)(2,1)S(1)}, u32[]{:S(2)}, u32[]{:S(2)}) collective-permute-start(bf16[256,128]{1,0:T(8,128)(2,1)S(1)} %get-tuple-element.969), channel_id=1, source_target_pairs={{4,0},{8,4},{12,8},{16,12},{20,16},{24,20},{28,24},{5,1},{9,5},{13... | collective-permute-start | bytes 196616 | tf_op jit(solution)/shard_map/ppermute | solution.py:14
  218.6 20.8 %collective-permute-start.12 = (bf16[4,256]{1,0:T(4,128)(2,1)S(1)}, bf16[4,256]{1,0:T(4,128)(2,1)S(1)}, u32[]{:S(2)}, u32[]{:S(2)}) collective-permute-start(bf16[4,256]{1,0:T(4,128)(2,1)S(1)} %get-tuple-element.975), channel_id=1, source_target_pairs={{4,0},{8,4},{12,8},{16,12},{20,16},{24,20},{28,24},{5,1},{9,5},{13... | collective-permute-start | bytes 6152 | tf_op jit(solution)/shard_map/ppermute | solution.py:14
  220.6 38.9 %collective-permute-start.13 = (bf16[4,256]{1,0:T(4,128)(2,1)S(1)}, bf16[4,256]{1,0:T(4,128)(2,1)S(1)}, u32[]{:S(2)}, u32[]{:S(2)}) collective-permute-start(bf16[4,256]{1,0:T(4,128)(2,1)S(1)} %get-tuple-element.979), channel_id=1, source_target_pairs={{8,0},{12,4},{16,8},{20,12},{24,16},{28,20},{9,1},{13,5},{17,9},{2... | collective-permute-start | bytes 6152 | tf_op jit(solution)/shard_map/ppermute | solution.py:14
  222.5 39.7 %collective-permute-start.14 = (bf16[4,256]{1,0:T(4,128)(2,1)S(1)}, bf16[4,256]{1,0:T(4,128)(2,1)S(1)}, u32[]{:S(2)}, u32[]{:S(2)}) collective-permute-start(bf16[4,256]{1,0:T(4,128)(2,1)S(1)} %get-tuple-element.978), channel_id=1, source_target_pairs={{12,0},{16,4},{20,8},{24,12},{28,16},{13,1},{17,5},{21,9},{25,13},... | collective-permute-start | bytes 6152 | tf_op jit(solution)/shard_map/ppermute | solution.py:14
  224.4 39.6 %collective-permute-start.15 = (bf16[4,256]{1,0:T(4,128)(2,1)S(1)}, bf16[4,256]{1,0:T(4,128)(2,1)S(1)}, u32[]{:S(2)}, u32[]{:S(2)}) collective-permute-start(bf16[4,256]{1,0:T(4,128)(2,1)S(1)} %get-tuple-element.977), channel_id=1, source_target_pairs={{16,0},{20,4},{24,8},{28,12},{17,1},{21,5},{25,9},{29,13},{18,2},{... | collective-permute-start | bytes 6152 | tf_op jit(solution)/shard_map/ppermute | solution.py:14
  229.3 39.4 %copy-start.7 = (bf16[1,4,256]{2,1,0:T(4,128)(2,1)S(1)}, bf16[1,4,256]{2,1,0:T(4,128)(2,1)}, u32[]{:S(2)}) copy-start(bf16[1,4,256]{2,1,0:T(4,128)(2,1)} %param.21) | copy-start | bytes 6148
  229.3 56.5 %copy-start.5 = (bf16[1,256,128]{2,1,0:T(8,128)(2,1)S(1)}, bf16[1,256,128]{2,1,0:T(8,128)(2,1)}, u32[]{:S(2)}) copy-start(bf16[1,256,128]{2,1,0:T(8,128)(2,1)} %param.19) | copy-start | bytes 196612
  229.3 56.5 %copy-start.8 = (f32[128]{0:T(128)S(1)}, f32[128]{0:T(128)}, u32[]{:S(2)}) copy-start(f32[128]{0:T(128)} %param.24) | copy-start | bytes 1540
  239.5 26.5 %collective-permute-start.16 = (bf16[4,256]{1,0:T(4,128)(2,1)S(1)}, bf16[4,256]{1,0:T(4,128)(2,1)S(1)}, u32[]{:S(2)}, u32[]{:S(2)}) collective-permute-start(bf16[4,256]{1,0:T(4,128)(2,1)S(1)} %get-tuple-element.976), channel_id=1, source_target_pairs={{20,0},{24,4},{28,8},{21,1},{25,5},{29,9},{22,2},{26,6},{30,10},{2... | collective-permute-start | bytes 6152 | tf_op jit(solution)/shard_map/ppermute | solution.py:14
  259.4 7.9 %collective-permute-start.17 = (bf16[4,256]{1,0:T(4,128)(2,1)S(1)}, bf16[4,256]{1,0:T(4,128)(2,1)S(1)}, u32[]{:S(2)}, u32[]{:S(2)}) collective-permute-start(bf16[4,256]{1,0:T(4,128)(2,1)S(1)} %get-tuple-element.980), channel_id=1, source_target_pairs={{24,0},{28,4},{25,1},{29,5},{26,2},{30,6},{27,3},{31,7}} | collective-permute-start | bytes 6152 | tf_op jit(solution)/shard_map/ppermute | solution.py:14
  262.1 9.6 %collective-permute-start.1 = (bf16[256,128]{1,0:T(8,128)(2,1)S(1)}, bf16[256,128]{1,0:T(8,128)(2,1)S(1)}, u32[]{:S(2)}, u32[]{:S(2)}) collective-permute-start(bf16[256,128]{1,0:T(8,128)(2,1)S(1)} %get-tuple-element.973), channel_id=1, source_target_pairs={{8,0},{12,4},{16,8},{20,12},{24,16},{28,20},{9,1},{13,5},{17,9},{2... | collective-permute-start | bytes 196616 | tf_op jit(solution)/shard_map/ppermute | solution.py:14
  264.1 10.3 %collective-permute-start.2 = (bf16[256,128]{1,0:T(8,128)(2,1)S(1)}, bf16[256,128]{1,0:T(8,128)(2,1)S(1)}, u32[]{:S(2)}, u32[]{:S(2)}) collective-permute-start(bf16[256,128]{1,0:T(8,128)(2,1)S(1)} %get-tuple-element.972), channel_id=1, source_target_pairs={{12,0},{16,4},{20,8},{24,12},{28,16},{13,1},{17,5},{21,9},{25,13},... | collective-permute-start | bytes 196616 | tf_op jit(solution)/shard_map/ppermute | solution.py:14
  266.0 10.6 %collective-permute-start.3 = (bf16[256,128]{1,0:T(8,128)(2,1)S(1)}, bf16[256,128]{1,0:T(8,128)(2,1)S(1)}, u32[]{:S(2)}, u32[]{:S(2)}) collective-permute-start(bf16[256,128]{1,0:T(8,128)(2,1)S(1)} %get-tuple-element.971), channel_id=1, source_target_pairs={{16,0},{20,4},{24,8},{28,12},{17,1},{21,5},{25,9},{29,13},{18,2},{... | collective-permute-start | bytes 196616 | tf_op jit(solution)/shard_map/ppermute | solution.py:14
  267.3 13.3 %collective-permute-start.4 = (bf16[256,128]{1,0:T(8,128)(2,1)S(1)}, bf16[256,128]{1,0:T(8,128)(2,1)S(1)}, u32[]{:S(2)}, u32[]{:S(2)}) collective-permute-start(bf16[256,128]{1,0:T(8,128)(2,1)S(1)} %get-tuple-element.970), channel_id=1, source_target_pairs={{20,0},{24,4},{28,8},{21,1},{25,5},{29,9},{22,2},{26,6},{30,10},{2... | collective-permute-start | bytes 196616 | tf_op jit(solution)/shard_map/ppermute | solution.py:14
  268.0 15.8 %collective-permute-start.5 = (bf16[256,128]{1,0:T(8,128)(2,1)S(1)}, bf16[256,128]{1,0:T(8,128)(2,1)S(1)}, u32[]{:S(2)}, u32[]{:S(2)}) collective-permute-start(bf16[256,128]{1,0:T(8,128)(2,1)S(1)} %get-tuple-element.974), channel_id=1, source_target_pairs={{24,0},{28,4},{25,1},{29,5},{26,2},{30,6},{27,3},{31,7}} | collective-permute-start | bytes 196616 | tf_op jit(solution)/shard_map/ppermute | solution.py:14
  271.8 15.8 %collective-permute-start.10 = (bf16[256,128]{1,0:T(8,128)(2,1)S(1)}, bf16[256,128]{1,0:T(8,128)(2,1)S(1)}, u32[]{:S(2)}, u32[]{:S(2)}) collective-permute-start(bf16[256,128]{1,0:T(8,128)(2,1)S(1)} %get-tuple-element.964), channel_id=1, source_target_pairs={{20,0},{24,4},{28,8},{21,1},{25,5},{29,9},{22,2},{26,6},{30,10},{2... | collective-permute-start | bytes 196616 | tf_op jit(solution)/shard_map/ppermute | solution.py:14
  274.4 57.5 %collective-permute-start.11 = (bf16[256,128]{1,0:T(8,128)(2,1)S(1)}, bf16[256,128]{1,0:T(8,128)(2,1)S(1)}, u32[]{:S(2)}, u32[]{:S(2)}) collective-permute-start(bf16[256,128]{1,0:T(8,128)(2,1)S(1)} %get-tuple-element.968), channel_id=1, source_target_pairs={{24,0},{28,4},{25,1},{29,5},{26,2},{30,6},{27,3},{31,7}} | collective-permute-start | bytes 196616 | tf_op jit(solution)/shard_map/ppermute | solution.py:14
  276.6 55.3 %collective-permute-start.6 = (bf16[256,128]{1,0:T(8,128)(2,1)S(1)}, bf16[256,128]{1,0:T(8,128)(2,1)S(1)}, u32[]{:S(2)}, u32[]{:S(2)}) collective-permute-start(bf16[256,128]{1,0:T(8,128)(2,1)S(1)} %get-tuple-element.963), channel_id=1, source_target_pairs={{4,0},{8,4},{12,8},{16,12},{20,16},{24,20},{28,24},{5,1},{9,5},{13... | collective-permute-start | bytes 196616 | tf_op jit(solution)/shard_map/ppermute | solution.py:14
  280.7 51.2 %collective-permute-start.7 = (bf16[256,128]{1,0:T(8,128)(2,1)S(1)}, bf16[256,128]{1,0:T(8,128)(2,1)S(1)}, u32[]{:S(2)}, u32[]{:S(2)}) collective-permute-start(bf16[256,128]{1,0:T(8,128)(2,1)S(1)} %get-tuple-element.967), channel_id=1, source_target_pairs={{8,0},{12,4},{16,8},{20,12},{24,16},{28,20},{9,1},{13,5},{17,9},{2... | collective-permute-start | bytes 196616 | tf_op jit(solution)/shard_map/ppermute | solution.py:14
  283.8 48.0 %collective-permute-start.8 = (bf16[256,128]{1,0:T(8,128)(2,1)S(1)}, bf16[256,128]{1,0:T(8,128)(2,1)S(1)}, u32[]{:S(2)}, u32[]{:S(2)}) collective-permute-start(bf16[256,128]{1,0:T(8,128)(2,1)S(1)} %get-tuple-element.966), channel_id=1, source_target_pairs={{12,0},{16,4},{20,8},{24,12},{28,16},{13,1},{17,5},{21,9},{25,13},... | collective-permute-start | bytes 196616 | tf_op jit(solution)/shard_map/ppermute | solution.py:14
  287.6 44.3 %collective-permute-start.9 = (bf16[256,128]{1,0:T(8,128)(2,1)S(1)}, bf16[256,128]{1,0:T(8,128)(2,1)S(1)}, u32[]{:S(2)}, u32[]{:S(2)}) collective-permute-start(bf16[256,128]{1,0:T(8,128)(2,1)S(1)} %get-tuple-element.965), channel_id=1, source_target_pairs={{16,0},{20,4},{24,8},{28,12},{17,1},{21,5},{25,9},{29,13},{18,2},{... | collective-permute-start | bytes 196616 | tf_op jit(solution)/shard_map/ppermute | solution.py:14
  (18 other events, 37.5 us)
where the time goes:
time: 335 us; the launch traced here: 333 us
  blocking collectives  128 us (38%)
  local copies, waits for them, and re-layouts  45.9 us (14%)
  matrix products  44.9 us (13%)
  waiting for transfers between devices  36.1 us (11%)
  loops' own time  28.8 us (9%)
  starting transfers between devices  28.5 us (9%)
  other arithmetic  19.3 us (6%)
    psum x1, blocking collectives, on_device(): lax.psum(jnp.stack([query_gain_part, key_gain_part]), ('seq', 'rep'))  42.9 us
    ppermute x18, waiting for transfers between devices, shifted(): lax.ppermute(value, axis, [(source, source + steps) for source in range(i...  36.1 us
    dot_general x16, matrix products, contract_first(): lax.dot_general(left_rows, right_rows, (((0,), (0,)), ((), ())), preferre...  30.9 us
    all_gather x1, blocking collectives, on_device(): lax.all_gather(key_normed, 'seq', axis=0, tiled=True)  29.4 us
    all_gather x1, blocking collectives, on_device(): lax.all_gather(value_local, 'seq', axis=0, tiled=True)  28.6 us
    ppermute x18, starting transfers between devices, shifted(): lax.ppermute(value, axis, [(source, source + steps) for source in range(i...  28.5 us
    all_gather x1, blocking collectives, on_device(): lax.all_gather(logit_local, 'seq', axis=1, tiled=True)  27.1 us
    another operation x1, loops' own time, on_device(): lax.scan(task_step, zero_parts, (query_tiles, grad_tiles, out_tiles, own_...  13.7 us
  transfers between devices with their start and end apart: 18, of which 6 were waited for; matrix products, arithmetic and copies ran while one was open for 4% of the time, Pallas kernels for 0%

commit v1 on v0

--- a/solution.py
+++ b/solution.py
@@ -2,6 +2,7 @@
 import jax.numpy as jnp
 from jax import lax
 from jax.sharding import PartitionSpec as P
+from jax.lax import axis_index, axis_size, ppermute
 
 TILE = 64
 norm_eps = 1e-06
@@ -233,6 +234,25 @@
 
 
 def on_device(queries, key_vectors, values, forget_logit, out_grad, query_gain, key_gain, lengths):
+
+    def _advance_works(x0):
+        known = axis_index("seq")
+        left_arr = axis_size("seq")
+        state_next, field_out = (left_arr, known)
+        big, before = (x0, 1)
+        while before < state_next:
+            arrivals = []
+            k0 = 0
+            while k0 < state_next:
+                arrivals.append((k0, k0 ^ before))
+                k0 += 1
+            local_out = ppermute(big, "seq", arrivals)
+            carry_out = jnp.concatenate([big, local_out], axis=0)
+            all_values = jnp.concatenate([local_out, big], axis=0)
+            big = jnp.where(field_out & before == 0, carry_out, all_values)
+            before = 2 * before
+        return big
+
     query_local = queries[0]
     key_local = key_vectors[0]
     value_local = values[0]
@@ -250,7 +270,7 @@
     key_normed = norm_rows(key_local, key_gain, 1.0).astype(jnp.bfloat16)
     pads = prepare(
         (
-            lax.all_gather(key_normed, "seq", axis=0, tiled=True),
+            _advance_works(key_normed),
             lax.all_gather(value_local, "seq", axis=0, tiled=True),
             lax.all_gather(logit_local, "seq", axis=1, tiled=True),
         )

time: 335 us -> 357 us (1.066)
  starting transfers between devices: 28.5 us -> 36.2 us
  blocking collectives: 128 us -> 133 us
  local copies, waits for them, and re-layouts: 45.9 us -> 49.6 us
    ppermute x0 -> x3, starting transfers between devices: none -> 7.7 us  [_advance_works(): local_out = ppermute(big, 'seq', arrivals)]
    ppermute x0 -> x3, waiting for transfers between devices: none -> 7.08 us  [_advance_works(): local_out = ppermute(big, 'seq', arrivals)]
    psum x1, blocking collectives: 42.9 us -> 47.9 us  [on_device(): lax.psum(jnp.stack([query_gain_part, key_gain_part]), ('seq', 'rep'))]
    ppermute x18, waiting for transfers between devices: 36.1 us -> 32 us  [shifted(): lax.ppermute(value, axis, [(source, source + steps) for source in range(i...]
  transfers between devices with their start and end apart: 18 -> 21, of which waited for: 6 -> 5; matrix products, arithmetic and copies ran while one was open for 4% -> 4% of each run, Pallas kernels for 0% -> 0%
where the time goes in v1:
time: 357 us; the launch traced here: 355 us
  blocking collectives  133 us (37%)
  local copies, waits for them, and re-layouts  49.6 us (14%)
  matrix products  44.9 us (13%)
  waiting for transfers between devices  39.1 us (11%)
  starting transfers between devices  36.2 us (10%)
  loops' own time  28.7 us (8%)
  other arithmetic  22.1 us (6%)
    psum x1, blocking collectives, on_device(): lax.psum(jnp.stack([query_gain_part, key_gain_part]), ('seq', 'rep'))  47.9 us
    ppermute x18, waiting for transfers between devices, shifted(): lax.ppermute(value, axis, [(source, source + steps) for source in range(i...  32 us
    dot_general x16, matrix products, contract_first(): lax.dot_general(left_rows, right_rows, (((0,), (0,)), ((), ())), preferre...  30.9 us
    all_gather x1, blocking collectives, on_device(): lax.all_gather(key_normed, 'seq', axis=0, tiled=True)  29.2 us
    all_gather x1, blocking collectives, on_device(): lax.all_gather(value_local, 'seq', axis=0, tiled=True)  28.8 us
    ppermute x18, starting transfers between devices, shifted(): lax.ppermute(value, axis, [(source, source + steps) for source in range(i...  28.5 us
    all_gather x1, blocking collectives, on_device(): lax.all_gather(logit_local, 'seq', axis=1, tiled=True)  27.6 us
    another operation x1, loops' own time, on_device(): lax.scan(task_step, zero_parts, (query_tiles, grad_tiles, out_tiles, own_...  13.7 us
  transfers between devices with their start and end apart: 21, of which 5 were waited for; matrix products, arithmetic and copies ran while one was open for 4% of the time, Pallas kernels for 0%

profile of v1, /device:TPU:12, one launch (start us, length us, event | category | flops | bytes accessed | tf_op | source)
XLA Modules:
  0.0 355.2 jit_solution(14973590054439431008)
XLA Ops:
  3.2 29.2 %all_gather.13 = bf16[2048,128]{1,0:T(8,128)(2,1)S(1)} all-gather(bf16[256,128]{1,0:T(8,128)(2,1)S(1)} %fusion.42), channel_id=1, replica_groups=mesh['seq'=8,'rep'=4] {'seq'}, dimensions={0}, use_global_device_ids=true | all-gather | bytes 589824 | tf_op jit(solution)/shard_map/all_gather | solution.py:298
  32.4 27.6 %all-gather = bf16[1,4,2048]{2,1,0:T(4,128)(2,1)S(1)} all-gather(bf16[1,4,256]{2,1,0:T(4,128)(2,1)} %param.21), channel_id=2, replica_groups=mesh['seq'=8,'rep'=4] {'seq'}, dimensions={2}, use_global_device_ids=true | all-gather | bytes 18432 | tf_op jit(solution)/shard_map/all_gather | solution.py:275
  61.4 28.8 %all-gather.1 = bf16[1,2048,128]{2,1,0:T(8,128)(2,1)S(1)} all-gather(bf16[1,256,128]{2,1,0:T(8,128)(2,1)} %param.20), channel_id=3, replica_groups=mesh['seq'=8,'rep'=4] {'seq'}, dimensions={1}, use_global_device_ids=true | all-gather | bytes 589824 | tf_op jit(solution)/shard_map/all_gather | solution.py:274
  90.5 3.7 %collective-permute-start.1 = (bf16[512,128]{1,0:T(8,128)(2,1)S(1)}, bf16[512,128]{1,0:T(8,128)(2,1)S(1)}, u32[]{:S(2)}, u32[]{:S(2)}) collective-permute-start(bf16[512,128]{1,0:T(8,128)(2,1)S(1)} %maximum_select_fusion.2), channel_id=1, source_target_pairs={{0,8},{4,12},{8,0},{12,4},{16,24},{20,28},{24,16},{28,20},{1,9},{5... | collective-permute-start | bytes 393224 | tf_op jit(solution)/shard_map/ppermute | solution.py:249
  94.4 2.7 collective-permute-done.1
  97.2 3.5 collective-permute-start.2
  102.4 4.4 %collective-permute-done.2 = bf16[1024,128]{1,0:T(8,128)(2,1)S(1)} collective-permute-done((bf16[1024,128]{1,0:T(8,128)(2,1)S(1)}, bf16[1024,128]{1,0:T(8,128)(2,1)S(1)}, u32[]{:S(2)}, u32[]{:S(2)}) %collective-permute-start.2) | collective-permute-done | bytes 262176 | tf_op jit(solution)/shard_map/ppermute | solution.py:249
  107.7 35.6 %while.166 = (s32[]{:T(128)}, bf16[4,64,512]{2,1,0:T(8,128)(2,1)}, s32[4]{0:T(128)S(1)}, s32[32]{0:T(128)S(1)}, bf16[4,64,512]{2,1,0:T(8,128)(2,1)S(1)}, /*index...) while((s32[]{:T(128)}, bf16[4,64,512]{2,1,0:T(8,128)(2,1)}, ...), condition=%wide.region_10.11_spmd, body=%wide.region_5.10_spmd.sunk | while | flops 68126688 | bytes 5365146 | solution.py:283
  112.8 2.9 while.170
  121.7 2.9 while.170
  130.6 2.9 while.170
  139.5 2.9 while.170
  145.7 87.9 %while.169 = (s32[]{:T(128)}, f32[2560,128]{1,0:T(8,128)}, f32[2560,128]{1,0:T(8,128)}, f32[4,2560]{1,0:T(4,128)S(1)}, bf16[4,64,512]{2,1,0:T(8,128)(2,1)S(1)}, ...) while((s32[]{:T(128)}, f32[2560,128]{1,0:T(8,128)}, ...), condition=%wide.region_21.22_spmd, body=%wide.region_11.21_spmd.sunk | while | flops 204607008 | bytes 11740149 | solution.py:326
  151.6 2.3 while.171
  156.1 11.2 %while.172 = (s32[]{:T(128)}, f32[2560,128]{1,0:T(8,128)}, f32[2560,128]{1,0:T(8,128)}, f32[4,2560]{1,0:T(4,128)S(1)}, f32[256,128]{1,0:T(8,128)S(1)}, /*index=5...) while((s32[]{:T(128)}, f32[2560,128]{1,0:T(8,128)}, ...), condition=%wide.wide.region_20.20_spmd, body=%wide.wide.region_17.19_spmd.sunk | while | flops 170100288 | bytes 6100827 | solution.py:218
  178.0 11.2 %while.172 = (s32[]{:T(128)}, f32[2560,128]{1,0:T(8,128)}, f32[2560,128]{1,0:T(8,128)}, f32[4,2560]{1,0:T(4,128)S(1)}, f32[256,128]{1,0:T(8,128)S(1)}, /*index=5...) while((s32[]{:T(128)}, f32[2560,128]{1,0:T(8,128)}, ...), condition=%wide.wide.region_20.20_spmd, body=%wide.wide.region_17.19_spmd.sunk | while | flops 170100288 | bytes 6100827 | solution.py:218
  195.5 2.3 while.171
  200.0 11.2 %while.172 = (s32[]{:T(128)}, f32[2560,128]{1,0:T(8,128)}, f32[2560,128]{1,0:T(8,128)}, f32[4,2560]{1,0:T(4,128)S(1)}, f32[256,128]{1,0:T(8,128)S(1)}, /*index=5...) while((s32[]{:T(128)}, f32[2560,128]{1,0:T(8,128)}, ...), condition=%wide.wide.region_20.20_spmd, body=%wide.wide.region_17.19_spmd.sunk | while | flops 170100288 | bytes 6100827 | solution.py:218
  217.5 2.3 while.171
  222.0 11.2 %while.172 = (s32[]{:T(128)}, f32[2560,128]{1,0:T(8,128)}, f32[2560,128]{1,0:T(8,128)}, f32[4,2560]{1,0:T(4,128)S(1)}, f32[256,128]{1,0:T(8,128)S(1)}, /*index=5...) while((s32[]{:T(128)}, f32[2560,128]{1,0:T(8,128)}, ...), condition=%wide.wide.region_20.20_spmd, body=%wide.wide.region_17.19_spmd.sunk | while | flops 170100288 | bytes 6100827 | solution.py:218
  253.3 14.0 %collective-permute-done.15 = bf16[4,256]{1,0:T(4,128)(2,1)S(1)} collective-permute-done((bf16[4,256]{1,0:T(4,128)(2,1)S(1)}, bf16[4,256]{1,0:T(4,128)(2,1)S(1)}, u32[]{:S(2)}, u32[]{:S(2)}) %collective-permute-start.15) | collective-permute-done | bytes 2080 | tf_op jit(solution)/shard_map/ppermute | solution.py:15
  267.9 15.9 %collective-permute-done.16 = bf16[4,256]{1,0:T(4,128)(2,1)S(1)} collective-permute-done((bf16[4,256]{1,0:T(4,128)(2,1)S(1)}, bf16[4,256]{1,0:T(4,128)(2,1)S(1)}, u32[]{:S(2)}, u32[]{:S(2)}) %collective-permute-start.16) | collective-permute-done | bytes 2080 | tf_op jit(solution)/shard_map/ppermute | solution.py:15
  293.8 5.2 %collective-permute-start.10 = (bf16[256,128]{1,0:T(8,128)(2,1)S(1)}, bf16[256,128]{1,0:T(8,128)(2,1)S(1)}, u32[]{:S(2)}, u32[]{:S(2)}) collective-permute-start(bf16[256,128]{1,0:T(8,128)(2,1)S(1)} %get-tuple-element.967), channel_id=1, source_target_pairs={{8,0},{12,4},{16,8},{20,12},{24,16},{28,20},{9,1},{13,5},{17,9},{2... | collective-permute-start | bytes 196616 | tf_op jit(solution)/shard_map/ppermute | solution.py:15
  306.7 47.9 %psum.7 = f32[2,128]{1,0:T(2,128)} all-reduce(f32[2,128]{1,0:T(2,128)S(1)} %pad_maximum_fusion), channel_id=1, replica_groups=mesh['seq'=8,'rep'=4] {'seq','rep'}, use_global_device_ids=true, to_apply=%region_30.31 | all-reduce | flops 256 | bytes 2048 | tf_op jit(solution)/shard_map/psum | solution.py:371
  (663 shorter events, 145.0 us)
Async XLA Ops:
  0.6 93.5 %copy-start.16 = (f32[128]{0:T(128)S(1)}, f32[128]{0:T(128)}, u32[]{:S(2)}) copy-start(f32[128]{0:T(128)} %param.23) | copy-start | bytes 1540
  0.6 93.5 %copy-start.15 = (s32[1,4]{1,0:T(1,128)S(1)}, s32[1,4]{1,0:T(1,128)}, u32[]{:S(2)}) copy-start(s32[1,4]{1,0:T(1,128)} %param.25) | copy-start | bytes 52
  0.7 100.0 %copy-start = (bf16[1,256,512]{2,1,0:T(8,128)(2,1)S(1)}, bf16[1,256,512]{2,1,0:T(8,128)(2,1)}, u32[]{:S(2)}) copy-start(bf16[1,256,512]{2,1,0:T(8,128)(2,1)} %param.18) | copy-start | bytes 786436
  2.6 87.8 %collective-permute-start = (bf16[256,128]{1,0:T(8,128)(2,1)S(1)}, bf16[256,128]{1,0:T(8,128)(2,1)S(1)}, u32[]{:S(2)}, u32[]{:S(2)}) collective-permute-start(bf16[256,128]{1,0:T(8,128)(2,1)S(1)} %fusion.42), channel_id=1, source_target_pairs={{0,4},{4,0},{8,12},{12,8},{16,20},{20,16},{24,28},{28,24},{1,5},{5... | collective-permute-start | bytes 196616 | tf_op jit(solution)/shard_map/ppermute | solution.py:249
  90.5 6.6 %collective-permute-start.1 = (bf16[512,128]{1,0:T(8,128)(2,1)S(1)}, bf16[512,128]{1,0:T(8,128)(2,1)S(1)}, u32[]{:S(2)}, u32[]{:S(2)}) collective-permute-start(bf16[512,128]{1,0:T(8,128)(2,1)S(1)} %maximum_select_fusion.2), channel_id=1, source_target_pairs={{0,8},{4,12},{8,0},{12,4},{16,24},{20,28},{24,16},{28,20},{1,9},{5... | collective-permute-start | bytes 393224 | tf_op jit(solution)/shard_map/ppermute | solution.py:249
  97.2 9.6 %collective-permute-start.2 = (bf16[1024,128]{1,0:T(8,128)(2,1)S(1)}, bf16[1024,128]{1,0:T(8,128)(2,1)S(1)}, u32[]{:S(2)}, u32[]{:S(2)}) collective-permute-start(bf16[1024,128]{1,0:T(8,128)(2,1)S(1)} %maximum_select_fusion.1), channel_id=1, source_target_pairs={{0,16},{4,20},{8,24},{12,28},{16,0},{20,4},{24,8},{28,12},{1,17},{... | collective-permute-start | bytes 786440 | tf_op jit(solution)/shard_map/ppermute | solution.py:249
  235.2 57.2 %collective-permute-start.3 = (bf16[256,128]{1,0:T(8,128)(2,1)S(1)}, bf16[256,128]{1,0:T(8,128)(2,1)S(1)}, u32[]{:S(2)}, u32[]{:S(2)}) collective-permute-start(bf16[256,128]{1,0:T(8,128)(2,1)S(1)} %get-tuple-element.969), channel_id=1, source_target_pairs={{4,0},{8,4},{12,8},{16,12},{20,16},{24,20},{28,24},{5,1},{9,5},{13... | collective-permute-start | bytes 196616 | tf_op jit(solution)/shard_map/ppermute | solution.py:15
  244.9 22.4 %collective-permute-start.15 = (bf16[4,256]{1,0:T(4,128)(2,1)S(1)}, bf16[4,256]{1,0:T(4,128)(2,1)S(1)}, u32[]{:S(2)}, u32[]{:S(2)}) collective-permute-start(bf16[4,256]{1,0:T(4,128)(2,1)S(1)} %get-tuple-element.975), channel_id=1, source_target_pairs={{4,0},{8,4},{12,8},{16,12},{20,16},{24,20},{28,24},{5,1},{9,5},{13... | collective-permute-start | bytes 6152 | tf_op jit(solution)/shard_map/ppermute | solution.py:15
  246.8 37.0 %collective-permute-start.16 = (bf16[4,256]{1,0:T(4,128)(2,1)S(1)}, bf16[4,256]{1,0:T(4,128)(2,1)S(1)}, u32[]{:S(2)}, u32[]{:S(2)}) collective-permute-start(bf16[4,256]{1,0:T(4,128)(2,1)S(1)} %get-tuple-element.979), channel_id=1, source_target_pairs={{8,0},{12,4},{16,8},{20,12},{24,16},{28,20},{9,1},{13,5},{17,9},{2... | collective-permute-start | bytes 6152 | tf_op jit(solution)/shard_map/ppermute | solution.py:15
  248.7 37.9 %collective-permute-start.17 = (bf16[4,256]{1,0:T(4,128)(2,1)S(1)}, bf16[4,256]{1,0:T(4,128)(2,1)S(1)}, u32[]{:S(2)}, u32[]{:S(2)}) collective-permute-start(bf16[4,256]{1,0:T(4,128)(2,1)S(1)} %get-tuple-element.978), channel_id=1, source_target_pairs={{12,0},{16,4},{20,8},{24,12},{28,16},{13,1},{17,5},{21,9},{25,13},... | collective-permute-start | bytes 6152 | tf_op jit(solution)/shard_map/ppermute | solution.py:15
  250.7 37.9 %collective-permute-start.18 = (bf16[4,256]{1,0:T(4,128)(2,1)S(1)}, bf16[4,256]{1,0:T(4,128)(2,1)S(1)}, u32[]{:S(2)}, u32[]{:S(2)}) collective-permute-start(bf16[4,256]{1,0:T(4,128)(2,1)S(1)} %get-tuple-element.977), channel_id=1, source_target_pairs={{16,0},{20,4},{24,8},{28,12},{17,1},{21,5},{25,9},{29,13},{18,2},{... | collective-permute-start | bytes 6152 | tf_op jit(solution)/shard_map/ppermute | solution.py:15
  267.2 23.2 %collective-permute-start.19 = (bf16[4,256]{1,0:T(4,128)(2,1)S(1)}, bf16[4,256]{1,0:T(4,128)(2,1)S(1)}, u32[]{:S(2)}, u32[]{:S(2)}) collective-permute-start(bf16[4,256]{1,0:T(4,128)(2,1)S(1)} %get-tuple-element.976), channel_id=1, source_target_pairs={{20,0},{24,4},{28,8},{21,1},{25,5},{29,9},{22,2},{26,6},{30,10},{2... | collective-permute-start | bytes 6152 | tf_op jit(solution)/shard_map/ppermute | solution.py:15
  283.8 8.0 %collective-permute-start.20 = (bf16[4,256]{1,0:T(4,128)(2,1)S(1)}, bf16[4,256]{1,0:T(4,128)(2,1)S(1)}, u32[]{:S(2)}, u32[]{:S(2)}) collective-permute-start(bf16[4,256]{1,0:T(4,128)(2,1)S(1)} %get-tuple-element.980), channel_id=1, source_target_pairs={{24,0},{28,4},{25,1},{29,5},{26,2},{30,6},{27,3},{31,7}} | collective-permute-start | bytes 6152 | tf_op jit(solution)/shard_map/ppermute | solution.py:15
  286.6 7.2 %collective-permute-start.4 = (bf16[256,128]{1,0:T(8,128)(2,1)S(1)}, bf16[256,128]{1,0:T(8,128)(2,1)S(1)}, u32[]{:S(2)}, u32[]{:S(2)}) collective-permute-start(bf16[256,128]{1,0:T(8,128)(2,1)S(1)} %get-tuple-element.973), channel_id=1, source_target_pairs={{8,0},{12,4},{16,8},{20,12},{24,16},{28,20},{9,1},{13,5},{17,9},{2... | collective-permute-start | bytes 196616 | tf_op jit(solution)/shard_map/ppermute | solution.py:15
  288.5 10.4 %collective-permute-start.5 = (bf16[256,128]{1,0:T(8,128)(2,1)S(1)}, bf16[256,128]{1,0:T(8,128)(2,1)S(1)}, u32[]{:S(2)}, u32[]{:S(2)}) collective-permute-start(bf16[256,128]{1,0:T(8,128)(2,1)S(1)} %get-tuple-element.972), channel_id=1, source_target_pairs={{12,0},{16,4},{20,8},{24,12},{28,16},{13,1},{17,5},{21,9},{25,13},... | collective-permute-start | bytes 196616 | tf_op jit(solution)/shard_map/ppermute | solution.py:15
  290.5 10.4 %collective-permute-start.6 = (bf16[256,128]{1,0:T(8,128)(2,1)S(1)}, bf16[256,128]{1,0:T(8,128)(2,1)S(1)}, u32[]{:S(2)}, u32[]{:S(2)}) collective-permute-start(bf16[256,128]{1,0:T(8,128)(2,1)S(1)} %get-tuple-element.971), channel_id=1, source_target_pairs={{16,0},{20,4},{24,8},{28,12},{17,1},{21,5},{25,9},{29,13},{18,2},{... | collective-permute-start | bytes 196616 | tf_op jit(solution)/shard_map/ppermute | solution.py:15
  291.8 10.4 %collective-permute-start.7 = (bf16[256,128]{1,0:T(8,128)(2,1)S(1)}, bf16[256,128]{1,0:T(8,128)(2,1)S(1)}, u32[]{:S(2)}, u32[]{:S(2)}) collective-permute-start(bf16[256,128]{1,0:T(8,128)(2,1)S(1)} %get-tuple-element.970), channel_id=1, source_target_pairs={{20,0},{24,4},{28,8},{21,1},{25,5},{29,9},{22,2},{26,6},{30,10},{2... | collective-permute-start | bytes 196616 | tf_op jit(solution)/shard_map/ppermute | solution.py:15
  292.5 10.4 %collective-permute-start.8 = (bf16[256,128]{1,0:T(8,128)(2,1)S(1)}, bf16[256,128]{1,0:T(8,128)(2,1)S(1)}, u32[]{:S(2)}, u32[]{:S(2)}) collective-permute-start(bf16[256,128]{1,0:T(8,128)(2,1)S(1)} %get-tuple-element.974), channel_id=1, source_target_pairs={{24,0},{28,4},{25,1},{29,5},{26,2},{30,6},{27,3},{31,7}} | collective-permute-start | bytes 196616 | tf_op jit(solution)/shard_map/ppermute | solution.py:15
  293.8 10.8 %collective-permute-start.10 = (bf16[256,128]{1,0:T(8,128)(2,1)S(1)}, bf16[256,128]{1,0:T(8,128)(2,1)S(1)}, u32[]{:S(2)}, u32[]{:S(2)}) collective-permute-start(bf16[256,128]{1,0:T(8,128)(2,1)S(1)} %get-tuple-element.967), channel_id=1, source_target_pairs={{8,0},{12,4},{16,8},{20,12},{24,16},{28,20},{9,1},{13,5},{17,9},{2... | collective-permute-start | bytes 196616 | tf_op jit(solution)/shard_map/ppermute | solution.py:15
  299.0 55.5 %collective-permute-start.11 = (bf16[256,128]{1,0:T(8,128)(2,1)S(1)}, bf16[256,128]{1,0:T(8,128)(2,1)S(1)}, u32[]{:S(2)}, u32[]{:S(2)}) collective-permute-start(bf16[256,128]{1,0:T(8,128)(2,1)S(1)} %get-tuple-element.966), channel_id=1, source_target_pairs={{12,0},{16,4},{20,8},{24,12},{28,16},{13,1},{17,5},{21,9},{25,13},... | collective-permute-start | bytes 196616 | tf_op jit(solution)/shard_map/ppermute | solution.py:15
  300.9 53.6 %collective-permute-start.12 = (bf16[256,128]{1,0:T(8,128)(2,1)S(1)}, bf16[256,128]{1,0:T(8,128)(2,1)S(1)}, u32[]{:S(2)}, u32[]{:S(2)}) collective-permute-start(bf16[256,128]{1,0:T(8,128)(2,1)S(1)} %get-tuple-element.965), channel_id=1, source_target_pairs={{16,0},{20,4},{24,8},{28,12},{17,1},{21,5},{25,9},{29,13},{18,2},{... | collective-permute-start | bytes 196616 | tf_op jit(solution)/shard_map/ppermute | solution.py:15
  302.2 52.3 %collective-permute-start.13 = (bf16[256,128]{1,0:T(8,128)(2,1)S(1)}, bf16[256,128]{1,0:T(8,128)(2,1)S(1)}, u32[]{:S(2)}, u32[]{:S(2)}) collective-permute-start(bf16[256,128]{1,0:T(8,128)(2,1)S(1)} %get-tuple-element.964), channel_id=1, source_target_pairs={{20,0},{24,4},{28,8},{21,1},{25,5},{29,9},{22,2},{26,6},{30,10},{2... | collective-permute-start | bytes 196616 | tf_op jit(solution)/shard_map/ppermute | solution.py:15
  302.9 51.6 %collective-permute-start.14 = (bf16[256,128]{1,0:T(8,128)(2,1)S(1)}, bf16[256,128]{1,0:T(8,128)(2,1)S(1)}, u32[]{:S(2)}, u32[]{:S(2)}) collective-permute-start(bf16[256,128]{1,0:T(8,128)(2,1)S(1)} %get-tuple-element.968), channel_id=1, source_target_pairs={{24,0},{28,4},{25,1},{29,5},{26,2},{30,6},{27,3},{31,7}} | collective-permute-start | bytes 196616 | tf_op jit(solution)/shard_map/ppermute | solution.py:15
  304.6 49.9 %collective-permute-start.9 = (bf16[256,128]{1,0:T(8,128)(2,1)S(1)}, bf16[256,128]{1,0:T(8,128)(2,1)S(1)}, u32[]{:S(2)}, u32[]{:S(2)}) collective-permute-start(bf16[256,128]{1,0:T(8,128)(2,1)S(1)} %get-tuple-element.963), channel_id=1, source_target_pairs={{4,0},{8,4},{12,8},{16,12},{20,16},{24,20},{28,24},{5,1},{9,5},{13... | collective-permute-start | bytes 196616 | tf_op jit(solution)/shard_map/ppermute | solution.py:15
  (27 other events, 418.5 us)
